TPU v7x, 512 devices: a whole 4x8x8 slice. The times are simulated.
512 devices in a mesh: row: 16 (over z, core), col: 32 (over y, x).
Axes of the slice: x: 4, y: 8, z: 8, core: 2. Of those that a mesh axis runs over, the one named last changes fastest.
Arguments:
- tokens: bfloat16 [4096, 2560], P('row', 'col'), may hold values from -6 to 6
- w_down: bfloat16 [2560, 1056], P('col'), may hold values from -0.125 to 0.125
- q_gain: float32 [768], replicated, may hold values from 0.1 to 1.9
- kv_gain: float32 [256], replicated, may hold values from 0.1 to 1.9
- w_q_up: bfloat16 [768, 3072], P(None, 'col'), may hold values from -8.8767604 to 8.8767604
- w_kv_up: bfloat16 [256, 4096], replicated, may hold values from -0.375 to 0.375
- w_out: bfloat16 [2048, 2560], P('col'), may hold values from -0.75 to 0.75
- latent_cache: bfloat16 [16, 8192, 288], P('row', 'col'), may hold values from -6 to 6
- cache_len: int32 [16], replicated, may hold values from 1 to 8192, as said below
- new_len: int32 [16], replicated, may hold values from 1 to 256, as said below
- page_table: int32 [16, 128], replicated, may hold values from 0 to 127, each once within a row
- home_slot: int32 [16], replicated, may hold values from 0 to 15, each once
Outputs:
- output: bfloat16 [4096, 2560], P('row', 'col')
Inputs may be any that keep to these rules, and one draw needn't show every extreme that they name: `cache_len`: some slot has exactly 8192 cached tokens; about half the slots hold at most 1024, the others at least 7168. `new_len`: some request has exactly 256 real new tokens.
All inputs are finite; a program needn't handle non-finite values.
Results may differ from a plain program's by a relative error of at most 0.023.
Values may be sent and summed in bfloat16 or wider, within the bound.
A program may use at most 64 MiB of HBM per device.

v0:
```python
import math
import jax
import jax.numpy as jnp
from jax import lax
from jax.sharding import PartitionSpec as P

NOPE = 64
ROPE = 32
VDIM = 64
epsilon = 1e-05


def rms_scale(values, gain):
    return values * lax.rsqrt(jnp.mean(values * values, axis=-1, keepdims=True) + epsilon) * gain


def angle_tables(positions, width):
    half_dim = width // 2
    frequency = 10000.0 ** (-2.0 * jnp.arange(half_dim, dtype=jnp.float32) / width)
    angles = positions.astype(jnp.float32)[:, None] * frequency[None, :]
    return (jnp.cos(angles), jnp.sin(angles))


def rotary(values, cosine, sine_table):
    half_dim = values.shape[-1] // 2
    first_half = values[..., :half_dim]
    second_half = values[..., half_dim:]
    return jnp.concatenate(
        [
            first_half * cosine - second_half * sine_table,
            second_half * cosine + first_half * sine_table,
        ],
        -1,
    )


def body(
    tokens,
    w_down,
    q_gain,
    kv_gain,
    w_q_up,
    w_kv_up,
    w_out,
    latent_cache,
    cache_len,
    new_len,
    page_table,
    home_slot,
):
    columns = lax.axis_size("col")
    column_id = lax.axis_index("col")
    row_id = lax.axis_index("row")
    group_rows = tokens.shape[0]
    own_rows = group_rows // columns
    q_width = q_gain.shape[0]
    kv_width = kv_gain.shape[0]
    slot_index = home_slot[row_id]
    cached_count = cache_len[slot_index]
    live_count = new_len[row_id]
    combined = lax.psum_scatter(
        jnp.dot(tokens, w_down, preferred_element_type=jnp.float32),
        "col",
        scatter_dimension=0,
        tiled=True,
    )
    own_position = cached_count + column_id * own_rows + jnp.arange(own_rows, dtype=jnp.int32)
    own_cos, own_sin = angle_tables(own_position, ROPE)
    query_latent = rms_scale(combined[:, :q_width], q_gain).astype(jnp.bfloat16)
    new_latent = rms_scale(combined[:, q_width : q_width + kv_width], kv_gain).astype(jnp.bfloat16)
    new_rope = rotary(combined[:, q_width + kv_width :], own_cos, own_sin).astype(jnp.bfloat16)
    new_rows = jnp.concatenate([new_latent, new_rope], 1)
    projected = jnp.dot(
        lax.all_gather(query_latent, "col", axis=0, tiled=True),
        w_q_up,
        preferred_element_type=jnp.float32,
    )
    query_cos, query_sin = angle_tables(
        cached_count + jnp.arange(group_rows, dtype=jnp.int32), ROPE
    )
    queries = jnp.concatenate(
        [projected[:, :NOPE], rotary(projected[:, NOPE:], query_cos, query_sin)], 1
    ).astype(jnp.bfloat16)
    segment = lax.all_gather(latent_cache, "row", axis=0, tiled=True)
    matches = jnp.arange(segment.shape[0], dtype=jnp.int32) == slot_index
    own_cache = jnp.sum(
        jnp.where(matches[:, None, None], segment.astype(jnp.float32), 0.0), 0
    ).astype(jnp.bfloat16)
    head_width = NOPE + VDIM
    head_weight = lax.dynamic_slice_in_dim(w_kv_up, column_id * head_width, head_width, 1)

    def expand(latents):
        lifted = jnp.dot(
            latents[:, :kv_width], head_weight, preferred_element_type=jnp.float32
        ).astype(jnp.bfloat16)
        return (jnp.concatenate([lifted[:, :NOPE], latents[:, kv_width:]], 1), lifted[:, NOPE:])

    cache_latents, fresh_latents = (
        lax.all_gather(own_cache, "col", axis=0, tiled=True),
        lax.all_gather(new_rows, "col", axis=0, tiled=True),
    )
    cache_keys, cache_values = expand(cache_latents)
    fresh_keys, fresh_values = expand(fresh_latents)
    key_total = cache_keys.shape[0]
    page_row = page_table[slot_index]
    page_count = page_row.shape[0]
    page_size = key_total // page_count
    block_size = min(512, key_total)
    offsets = jnp.arange(page_size, dtype=jnp.int32)
    page_ids = jnp.arange(page_count, dtype=jnp.int32)
    logical_page = jnp.sum(
        page_ids[:, None] * (page_row[:, None] == page_ids[None, :]).astype(jnp.int32), 0
    )
    cached_visible = (logical_page[:, None] * page_size + offsets[None, :]).reshape(
        key_total
    ) < cached_count
    block_limit = key_total // block_size
    score_scale = 1.0 / math.sqrt(NOPE + ROPE)
    query_index = jnp.arange(group_rows, dtype=jnp.int32)[:, None]
    key_index = jnp.arange(group_rows, dtype=jnp.int32)[None, :]
    fresh_visible = (key_index <= query_index) & (key_index < live_count)
    fresh_scores = (
        jnp.einsum("qd,kd->qk", queries, fresh_keys, preferred_element_type=jnp.float32)
        * score_scale
    )
    fresh_scores = jnp.where(fresh_visible, fresh_scores, -jnp.inf)
    first_peak = jnp.max(fresh_scores, 1)
    fresh_exponent = jnp.exp(fresh_scores - first_peak[:, None])
    start_state = (
        first_peak,
        jnp.sum(fresh_exponent, 1),
        jnp.dot(
            fresh_exponent.astype(jnp.bfloat16), fresh_values, preferred_element_type=jnp.float32
        ),
    )

    def accumulate(block_id, running):
        row_peak, row_total, summed = running
        key_block = lax.dynamic_slice_in_dim(cache_keys, block_id * block_size, block_size, 0)
        mask_block = lax.dynamic_slice_in_dim(cached_visible, block_id * block_size, block_size, 0)
        value_block = lax.dynamic_slice_in_dim(cache_values, block_id * block_size, block_size, 0)
        raw_scores = (
            jnp.einsum("qd,kd->qk", queries, key_block, preferred_element_type=jnp.float32)
            * score_scale
        )
        raw_scores = jnp.where(mask_block[None, :], raw_scores, -jnp.inf)
        next_peak = jnp.maximum(row_peak, jnp.max(raw_scores, 1))
        factor = jnp.exp(row_peak - next_peak)
        exponent = jnp.exp(raw_scores - next_peak[:, None])
        next_total = row_total * factor + jnp.sum(exponent, 1)
        next_summed = summed * factor[:, None] + jnp.dot(
            exponent.astype(jnp.bfloat16), value_block, preferred_element_type=jnp.float32
        )
        return (next_peak, next_total, next_summed)

    row_peak, row_total, summed = lax.fori_loop(0, block_limit, accumulate, start_state)
    attended = (summed / row_total[:, None]).astype(jnp.bfloat16)
    live_rows = jnp.arange(group_rows, dtype=jnp.int32) < live_count
    attended = jnp.where(live_rows[:, None], attended, jnp.zeros_like(attended))
    summed_out = lax.psum_scatter(
        lax.dot_general(
            w_out, attended, (((0,), (1,)), ((), ())), preferred_element_type=jnp.float32
        ).astype(jnp.bfloat16),
        "col",
        scatter_dimension=0,
        tiled=True,
    ).astype(jnp.float32)
    result = summed_out.T.astype(jnp.bfloat16)
    return result


def solution(mesh):
    return jax.shard_map(
        body,
        mesh=mesh,
        in_specs=(
            P("row", "col"),
            P("col", None),
            P(),
            P(),
            P(None, "col"),
            P(),
            P("col", None),
            P("row", "col", None),
            P(),
            P(),
            P(),
            P(),
        ),
        out_specs=P("row", "col"),
        check_vma=False,
    )
```

profile of v0, /device:TPU:16, one launch (start us, length us, event | category | flops | bytes accessed | tf_op | source)
XLA Modules:
  0.0 535.3 jit_solution(15060410855748943424)
XLA Ops:
  8.1 2.3 fusion.51
  11.9 46.3 %all-gather.3.cloned.1.call-done = bf16[16,256,288]{1,2,0:T(8,128)(2,1)} async-done(((bf16[1,256,288]{1,2,0:T(8,128)(2,1)}), bf16[16,256,288]{1,2,0:T(8,128)(2,1)}) %all-gather.3.cloned.1.call-update) | async-done | bytes 2359312 | tf_op jit(solution)/shard_map/all_gather | solution.py:84
  58.2 2.9 select_reduce_fusion
  66.8 1.3 dynamic-slice
  70.1 106.5 %all-reduce.3.cloned.1.call-done = f32[256,1056]{1,0:T(8,128)} async-done(((f32[256,1056]{1,0:T(8,128)}), f32[256,1056]{1,0:T(8,128)}) %all-reduce.3.cloned.1.call-update) | async-done | bytes 1081360
  179.2 44.2 %all_gather.13 = bf16[256,288]{1,0:T(8,128)(2,1)S(1)} all-gather(bf16[8,288]{1,0:T(8,128)(2,1)S(1)} %pad_maximum_fusion.2), channel_id=1, replica_groups=mesh['row'=16,'col'=32] {'col'}, dimensions={0}, use_global_device_ids=true | all-gather | bytes 152064 | tf_op jit(solution)/shard_map/all_gather | solution.py:100
  225.4 46.8 %all_gather.12 = bf16[256,768]{1,0:T(8,128)(2,1)S(1)} all-gather(bf16[8,768]{1,0:T(8,128)(2,1)S(1)} %multiply_convert_fusion), channel_id=1, replica_groups=mesh['row'=16,'col'=32] {'col'}, dimensions={0}, use_global_device_ids=true | all-gather | bytes 405504 | tf_op jit(solution)/shard_map/all_gather | solution.py:74
  273.3 3.0 convolution_convert_fusion
  277.3 1.3 pad_maximum_fusion
  278.6 26.9 %while.17 = (s32[]{:T(128)}, f32[256]{0:T(256)S(1)}, f32[256]{0:T(256)S(1)}, f32[256,64]{0,1:T(8,128)S(1)}, pred[8192]{0:T(1024)(128)(4,1)S(1)}, /*index=5*/bf16...) while((s32[]{:T(128)}, f32[256]{0:T(256)S(1)}, ...), condition=%wide.region_10.11_spmd, body=%wide.region_7.10_spmd.sunk | while | flops 42893828 | bytes 1935023 | solution.py:156
  280.3 1.2 fusion.67
  282.0 1.2 fusion.67
  283.7 1.2 fusion.67
  285.4 1.2 fusion.67
  287.1 1.2 fusion.67
  288.7 1.2 fusion.67
  290.4 1.2 fusion.67
  292.1 1.2 fusion.67
  295.5 1.2 fusion.67
  298.8 1.2 fusion.67
  302.2 1.2 fusion.67
  305.5 1.5 fusion.10
  307.0 1.5 copy.43
  308.5 219.2 %reduce-scatter.4.cloned.1.call-done = bf16[80,256]{1,0:T(8,128)(2,1)} async-done(((bf16[2560,256]{1,0:T(8,128)(2,1)}), bf16[80,256]{1,0:T(8,128)(2,1)}) %reduce-scatter.4.cloned.1.call-update) | async-done | bytes 40976
  (160 shorter events, 26.5 us)
Async XLA Ops:
  7.4 216.1 %copy-start = (bf16[256,4096]{1,0:T(8,128)(2,1)S(1)}, bf16[256,4096]{1,0:T(8,128)(2,1)}, u32[]{:S(2)}) copy-start(bf16[256,4096]{1,0:T(8,128)(2,1)} %param.19) | copy-start | bytes 6291460
  7.4 3.2 copy-start.4
  7.4 50.8 %all-gather.3.cloned.1.call-start = ((), (), s32[]{:S(2)}) async-start(), calls=%async_computation.1 | async-start | bytes 2506752 | tf_op jit(solution)/shard_map/all_gather | solution.py:84
  8.1 168.5 %all-reduce.3.cloned.1.call-start = ((), (), s32[]{:S(2)}) async-start(), calls=%async_computation.4 | async-start | bytes 2359296
  10.5 52.0 %copy-start.5 = (s32[16]{0:T(128)S(1)}, s32[16]{0:T(128)}, u32[]{:S(2)}) copy-start(s32[16]{0:T(128)} %param.23) | copy-start | bytes 196
  10.5 53.4 %copy-start.6 = (s32[16]{0:T(128)S(1)}, s32[16]{0:T(128)}, u32[]{:S(2)}) copy-start(s32[16]{0:T(128)} %param.22) | copy-start | bytes 196
  10.5 167.9 %copy-start.3 = (f32[256]{0:T(256)S(1)}, f32[256]{0:T(256)}, u32[]{:S(2)}) copy-start(f32[256]{0:T(256)} %param.17) | copy-start | bytes 3076
  10.5 214.1 %copy-start.2 = (f32[768]{0:T(1024)S(1)}, f32[768]{0:T(1024)}, u32[]{:S(2)}) copy-start(f32[768]{0:T(1024)} %param.16) | copy-start | bytes 9220
  10.5 261.7 %copy-start.1 = (bf16[768,96]{0,1:T(8,128)(2,1)S(1)}, bf16[768,96]{0,1:T(8,128)(2,1)}, u32[]{:S(2)}) copy-start(bf16[768,96]{0,1:T(8,128)(2,1)} %param.18) | copy-start | bytes 442372
  10.5 262.8 %all-gather.5.cloned.1.call-start = ((), (), s32[]{:S(2)}) async-start(), calls=%async_computation.2 | async-start | bytes 4866048 | tf_op jit(solution)/shard_map/all_gather | solution.py:99
  61.1 466.6 %reduce-scatter.4.cloned.1.call-start = ((), (), s32[]{:S(2)}) async-start(), calls=%async_computation.3 | async-start | bytes 1351680
  276.3 1.0 slice-start
Sparse Core Ops, SparseCore 0:
  10.3 47.8 all-gather.2
Sparse Core Ops, SparseCore 1:
  12.0 164.5 all-reduce.2
  179.5 89.1 all-gather.4
  308.6 219.1 reduce-scatter.3
where the time goes:
time: 536 us; the launch traced here: 535 us
  waiting for transfers between devices  373 us (70%)
  blocking collectives  91 us (17%)
  matrix products  30.2 us (6%)
  between operations  18.6 us (3%)
  other arithmetic  13.9 us (3%)
  local copies, waits for them, and re-layouts  8.05 us (2%)
    unnamed x6, waiting for transfers between devices  326 us
    all_gather x1, blocking collectives, body(): lax.all_gather(query_latent, 'col', axis=0, tiled=True)  46.8 us
    all_gather x1, waiting for transfers between devices, body(): segment = lax.all_gather(latent_cache, 'row', axis=0, tiled=True)  46.3 us
    all_gather x1, blocking collectives, body(): lax.all_gather(new_rows, 'col', axis=0, tiled=True)  44.2 us
    dot_general x16, matrix products, accumulate(): jnp.einsum('qd,kd->qk', queries, key_block, preferred_element_type=jnp.fl...  18.8 us
  transfers between devices with their start and end apart: 4, of which 3 were waited for; matrix products, arithmetic and copies ran while one was open for 3% of the time, Pallas kernels for 0%

commit v1 on v0

--- a/solution.py
+++ b/solution.py
@@ -8,6 +8,21 @@
 ROPE = 32
 VDIM = 64
 epsilon = 1e-05
+
+
+def cards_time(x_part, device_axis):
+    n = lax.axis_size(device_axis)
+    runs = [(pp, (pp + 1) % n) for pp in range(n)]
+
+    def fix_sites_over_axis(k_now):
+        if len(k_now) == n:
+            return k_now
+        return fix_sites_over_axis(
+            [lax.ppermute(k_now[0], axis_name=device_axis, perm=runs), *k_now]
+        )
+
+    e_now = jnp.concatenate(fix_sites_over_axis([x_part]), axis=0)
+    return jnp.roll(e_now, (lax.axis_index(device_axis) + 1) * x_part.shape[0], axis=0)
 
 
 def rms_scale(values, gain):
@@ -81,7 +96,7 @@
     queries = jnp.concatenate(
         [projected[:, :NOPE], rotary(projected[:, NOPE:], query_cos, query_sin)], 1
     ).astype(jnp.bfloat16)
-    segment = lax.all_gather(latent_cache, "row", axis=0, tiled=True)
+    segment = cards_time(latent_cache, "row")
     matches = jnp.arange(segment.shape[0], dtype=jnp.int32) == slot_index
     own_cache = jnp.sum(
         jnp.where(matches[:, None, None], segment.astype(jnp.float32), 0.0), 0

time: 536 us -> 620 us (1.16)
  waiting for transfers between devices: 373 us -> 445 us
  local copies, waits for them, and re-layouts: 8.05 us -> 20.6 us
    ppermute x0 -> x15, waiting for transfers between devices: none -> 88.3 us  [fix_sites_over_axis(): lax.ppermute(k_now[0], axis_name=device_axis, perm=runs)]
    all_gather x1 -> x0, waiting for transfers between devices: 46.3 us -> none  [body(): segment = lax.all_gather(latent_cache, 'row', axis=0, tiled=True)]
    unnamed x6 -> x5, waiting for transfers between devices: 326 us -> 357 us
    unnamed x17 -> x66, local copies, waits for them, and re-layouts: 2.84 us -> 14.7 us
  transfers between devices with their start and end apart: 4 -> 18, of which waited for: 3 -> 17; matrix products, arithmetic and copies ran while one was open for 3% -> 4% of each run, Pallas kernels for 0% -> 0%
where the time goes in v1:
time: 620 us; the launch traced here: 618 us
  waiting for transfers between devices  445 us (72%)
  blocking collectives  90.9 us (15%)
  matrix products  31.1 us (5%)
  local copies, waits for them, and re-layouts  20.6 us (3%)
  between operations  16.9 us (3%)
  other arithmetic  12.3 us (2%)
    unnamed x5, waiting for transfers between devices  357 us
    ppermute x15, waiting for transfers between devices, fix_sites_over_axis(): lax.ppermute(k_now[0], axis_name=device_axis, perm=runs)  88.3 us
    all_gather x1, blocking collectives, body(): lax.all_gather(query_latent, 'col', axis=0, tiled=True)  47 us
    all_gather x1, blocking collectives, body(): lax.all_gather(new_rows, 'col', axis=0, tiled=True)  43.9 us
    dot_general x16, matrix products, accumulate(): jnp.einsum('qd,kd->qk', queries, key_block, preferred_element_type=jnp.fl...  18.8 us
    unnamed x66, local copies, waits for them, and re-layouts  14.7 us
  transfers between devices with their start and end apart: 18, of which 17 were waited for; matrix products, arithmetic and copies ran while one was open for 4% of the time, Pallas kernels for 0%

profile of v1, /device:TPU:16, one launch (start us, length us, event | category | flops | bytes accessed | tf_op | source)
XLA Modules:
  0.0 618.2 jit_solution(9066850102167750559)
XLA Ops:
  6.6 11.5 %collective-permute-done = bf16[1,256,288]{1,2,0:T(8,128)(2,1)S(1)} collective-permute-done((bf16[1,256,288]{1,2,0:T(8,128)(2,1)}, bf16[1,256,288]{1,2,0:T(8,128)(2,1)S(1)}, u32[]{:S(2)}, u32[]{:S(2)}) %collective-permute-start) | collective-permute-done | bytes 147488 | tf_op jit(solution)/shard_map/ppermute | solution.py:21
  18.1 5.8 collective-permute-done.1
  23.9 5.8 collective-permute-done.2
  29.6 5.8 collective-permute-done.3
  35.4 5.8 collective-permute-done.4
  41.2 5.8 collective-permute-done.5
  47.0 5.8 collective-permute-done.6
  52.8 5.8 collective-permute-done.7
  58.5 5.8 collective-permute-done.8
  65.0 5.8 collective-permute-done.9
  71.4 5.8 collective-permute-done.10
  77.9 5.8 collective-permute-done.11
  84.3 5.8 collective-permute-done.12
  90.7 5.9 collective-permute-done.13
  96.6 2.3 fusion.52
  101.2 1.6 collective-permute-done.14
  121.8 136.7 %all-reduce.3.cloned.1.call-done = f32[256,1056]{1,0:T(8,128)} async-done(((f32[256,1056]{1,0:T(8,128)}), f32[256,1056]{1,0:T(8,128)}) %all-reduce.3.cloned.1.call-update) | async-done | bytes 1081360
  261.1 43.9 %all_gather.10 = bf16[256,288]{1,0:T(8,128)(2,1)S(1)} all-gather(bf16[8,288]{1,0:T(8,128)(2,1)S(1)} %pad_maximum_fusion.2), channel_id=1, replica_groups=mesh['row'=16,'col'=32] {'col'}, dimensions={0}, use_global_device_ids=true | all-gather | bytes 152064 | tf_op jit(solution)/shard_map/all_gather | solution.py:115
  307.1 47.0 %all_gather.9 = bf16[256,768]{1,0:T(8,128)(2,1)S(1)} all-gather(bf16[8,768]{1,0:T(8,128)(2,1)S(1)} %multiply_convert_fusion), channel_id=1, replica_groups=mesh['row'=16,'col'=32] {'col'}, dimensions={0}, use_global_device_ids=true | all-gather | bytes 405504 | tf_op jit(solution)/shard_map/all_gather | solution.py:89
  356.1 3.0 convolution_convert_fusion
  361.4 26.9 %while.17 = (s32[]{:T(128)}, f32[256]{0:T(256)S(1)}, f32[256]{0:T(256)S(1)}, f32[256,64]{0,1:T(8,128)S(1)}, pred[8192]{0:T(1024)(128)(4,1)S(1)}, /*index=5*/bf16...) while((s32[]{:T(128)}, f32[256]{0:T(256)S(1)}, ...), condition=%wide.region_10.11_spmd, body=%wide.region_7.10_spmd.sunk | while | flops 42893828 | bytes 1935023 | solution.py:171
  388.3 1.5 fusion.10
  389.8 1.4 copy.43
  391.3 220.3 %reduce-scatter.4.cloned.1.call-done = bf16[80,256]{1,0:T(8,128)(2,1)} async-done(((bf16[2560,256]{1,0:T(8,128)(2,1)}), bf16[80,256]{1,0:T(8,128)(2,1)}) %reduce-scatter.4.cloned.1.call-update) | async-done | bytes 40976
  (237 shorter events, 56.0 us)
Async XLA Ops:
  6.5 298.5 %copy-start = (bf16[256,4096]{1,0:T(8,128)(2,1)S(1)}, bf16[256,4096]{1,0:T(8,128)(2,1)}, u32[]{:S(2)}) copy-start(bf16[256,4096]{1,0:T(8,128)(2,1)} %param.19) | copy-start | bytes 6291460
  6.5 102.9 %copy-start.1 = (bf16[1,256,288]{1,2,0:T(8,128)(2,1)S(1)}, bf16[1,256,288]{1,2,0:T(8,128)(2,1)}, u32[]{:S(2)}) copy-start(bf16[1,256,288]{1,2,0:T(8,128)(2,1)} %param.21) | copy-start | bytes 442372
  6.5 252.0 %all-reduce.3.cloned.1.call-start = ((), (), s32[]{:S(2)}) async-start(), calls=%async_computation.3 | async-start | bytes 2359296
  6.5 11.5 %collective-permute-start = (bf16[1,256,288]{1,2,0:T(8,128)(2,1)}, bf16[1,256,288]{1,2,0:T(8,128)(2,1)S(1)}, u32[]{:S(2)}, u32[]{:S(2)}) collective-permute-start(bf16[1,256,288]{1,2,0:T(8,128)(2,1)} %param.21), channel_id=1, source_target_pairs={{0,32},{32,64},{64,96},{96,128},{128,160},{160,192},{192,224},{224... | collective-permute-start | bytes 442376 | tf_op jit(solution)/shard_map/ppermute | solution.py:21
  18.1 5.8 collective-permute-start.1
  23.9 5.8 collective-permute-start.2
  29.6 5.8 collective-permute-start.3
  35.4 5.8 collective-permute-start.4
  41.2 5.8 collective-permute-start.5
  47.0 5.8 collective-permute-start.6
  52.8 5.8 collective-permute-start.7
  58.5 5.8 collective-permute-start.8
  65.0 5.8 collective-permute-start.9
  71.4 5.8 collective-permute-start.10
  77.9 5.8 collective-permute-start.11
  84.3 5.8 collective-permute-start.12
  90.7 5.9 collective-permute-start.13
  96.6 6.1 collective-permute-start.14
  99.0 257.1 %all-gather.2.cloned.1.call-start = ((), (), s32[]{:S(2)}) async-start(), calls=%async_computation.1 | async-start | bytes 4866048 | tf_op jit(solution)/shard_map/all_gather | solution.py:114
  99.1 12.3 %copy-start.5 = (bf16[1,256,288]{1,2,0:T(8,128)(2,1)S(1)}, bf16[1,256,288]{1,2,0:T(8,128)(2,1)}, u32[]{:S(2)}) copy-start(bf16[1,256,288]{1,2,0:T(8,128)(2,1)} %copy-done.4) | copy-start | bytes 442372
  99.1 12.3 %copy-start.3 = (bf16[1,256,288]{1,2,0:T(8,128)(2,1)S(1)}, bf16[1,256,288]{1,2,0:T(8,128)(2,1)}, u32[]{:S(2)}) copy-start(bf16[1,256,288]{1,2,0:T(8,128)(2,1)} %copy-done.2) | copy-start | bytes 442372
  109.3 151.0 %copy-start.13 = (f32[256]{0:T(256)S(1)}, f32[256]{0:T(256)}, u32[]{:S(2)}) copy-start(f32[256]{0:T(256)} %param.17) | copy-start | bytes 3076
  109.3 196.9 %copy-start.12 = (f32[768]{0:T(1024)S(1)}, f32[768]{0:T(1024)}, u32[]{:S(2)}) copy-start(f32[768]{0:T(1024)} %param.16) | copy-start | bytes 9220
  112.8 498.8 %reduce-scatter.4.cloned.1.call-start = ((), (), s32[]{:S(2)}) async-start(), calls=%async_computation.2 | async-start | bytes 1351680
  (11 other events, 52.4 us)
Sparse Core Ops, SparseCore 0:
  99.1 159.3 all-reduce.2
  261.5 89.9 all-gather.1
  391.4 220.1 reduce-scatter.3
